TPU v7x, 32 devices: a whole 2x2x4 slice. The times are simulated.
32 devices in a mesh: grp: 2 (over y), dev: 8 (over z, core), pair: 2 (over x), sub: 1.
Axes of the slice: x: 2, y: 2, z: 4, core: 2. Of those that a mesh axis runs over, the one named last changes fastest.
Arguments:
- queries: bfloat16 [256, 4096], P(('grp', 'dev', 'sub'), 'pair'), parts along dimension 0, may hold values from -6 to 6
- key_rows: bfloat16 [256, 4096], P(('grp', 'dev', 'sub'), 'pair'), parts along dimension 0, may hold values from -6 to 6
- value_rows: bfloat16 [256, 4096], P(('grp', 'dev', 'sub'), 'pair'), parts along dimension 0, may hold values from -6 to 6
- states: float32 [64, 32, 128, 128], P(('grp', 'dev', 'sub'), 'pair'), parts along dimension 0, may hold values from -6 to 6
- decay_rates: float32 [32], P('pair'), may hold values from 0.02 to 2
- head_gain: float32 [4096], P('pair'), may hold values from 0.5 to 1.5
- out_weight: bfloat16 [4096, 6144], P('pair', ('dev', 'sub')), may hold values from -0.09375 to 0.09375
- residual: bfloat16 [256, 6144], P(('grp', 'dev', 'pair', 'sub')), parts along dimension 0, may hold values from -6 to 6
- norm_gain: float32 [6144], replicated, may hold values from 0.5 to 1.5
- expert_ids: int32 [256, 2], P(('grp', 'dev', 'pair', 'sub')), parts along dimension 0, may hold values from 0 to 3, all different within a row; in each aligned block of 8 rows (0 to 7, 8 to 15, ...) at most 4 rows name the same one
- gate_weights: float32 [256, 2], P(('grp', 'dev', 'pair', 'sub')), parts along dimension 0, may hold values from 0.1 to 1
- expert_gate: bfloat16 [18432, 6144], P(('dev', 'pair', 'sub')), may hold values from -0.078125 to 0.078125
- expert_up: bfloat16 [18432, 6144], P(('dev', 'pair', 'sub')), may hold values from -0.078125 to 0.078125
- expert_down: bfloat16 [18432, 6144], P(('dev', 'pair', 'sub')), may hold values from -0.09375 to 0.09375
Outputs:
- layer_out: bfloat16 [256, 6144], P(('grp', 'dev', 'pair', 'sub')), parts along dimension 0
There are 2 independent parts, one for each index of `grp`. A program takes and returns all parts, laid end to end along the dimension named above; an argument that names none is the same for every part. Nothing has to cross between parts.
Inputs may be any that keep to these rules, and one draw needn't show every extreme that they name: `expert_ids`: each row names 2 different experts. In each aligned block of 8 rows (the rows of one device) no expert is named by more than 4 rows, and in every draw some block has an expert named by exactly 4 rows.
All inputs are finite; a program needn't handle non-finite values.
Results may differ from a plain program's by a relative error of at most 0.0048.
Values may be sent and summed in bfloat16 or wider, within the bound.
A program may use at most 128 MiB of HBM per device.

v0:
```python
import jax
import jax.numpy as jnp
from jax import lax
from jax.sharding import PartitionSpec as P

EPSILON = 1e-06
HIGHEST = lax.Precision.HIGHEST


def attend(queries, key_rows, value_rows, states, decay_rates, head_gain):
    requests = states.shape[0]
    head_count = states.shape[1]
    head_size = states.shape[2]
    positions = queries.shape[0] // requests
    layout = (requests, positions, head_count, head_size)
    query_plain = queries.reshape(layout)
    key_plain = key_rows.reshape(layout)
    query_float = query_plain.astype(jnp.float32)
    value_float = value_rows.reshape(layout).astype(jnp.float32)
    offsets = jnp.arange(positions, dtype=jnp.float32)
    carried = jnp.exp(-decay_rates[None, :] * (offsets[:, None] + 1.0))
    from_state = jnp.einsum("rphk,rhkv->rphv", query_float, states, precision=HIGHEST)
    from_state = from_state * carried[None, :, :, None]
    scores = jnp.einsum(
        "rthk,rjhk->rhtj", query_plain, key_plain, preferred_element_type=jnp.float32
    )
    distance = offsets[:, None] - offsets[None, :]
    fading = jnp.exp(-decay_rates[:, None, None] * jnp.maximum(distance, 0.0)[None, :, :])
    fading = jnp.where(distance[None, :, :] >= 0.0, fading, 0.0)
    scores = scores * fading[None]
    within = jnp.einsum("rhtj,rjhv->rthv", scores, value_float, precision=HIGHEST)
    mixed_heads = from_state + within
    spread = jnp.mean(mixed_heads * mixed_heads, axis=3, keepdims=True)
    normal = (
        mixed_heads
        * lax.rsqrt(spread + EPSILON)
        * head_gain.reshape(head_count, head_size)[None, None]
    )
    return normal.astype(jnp.bfloat16).reshape(requests * positions, head_count * head_size)


def expert_apply(picked, gate_part, up_part, down_part):
    leading = picked.shape
    flattened = picked.reshape(-1, leading[-1])
    contract = (((1,), (1,)), ((), ()))
    gate_value = lax.dot_general(flattened, gate_part, contract, preferred_element_type=jnp.float32)
    lifted = lax.dot_general(flattened, up_part, contract, preferred_element_type=jnp.float32)
    hidden = (jax.nn.silu(gate_value) * lifted).astype(jnp.bfloat16)
    output = jnp.dot(hidden, down_part, preferred_element_type=jnp.float32)
    return output.reshape(leading)


def on_device(
    queries,
    key_rows,
    value_rows,
    states,
    decay_rates,
    head_gain,
    out_weight,
    residual,
    norm_gain,
    expert_ids,
    gate_weights,
    expert_gate,
    expert_up,
    expert_down,
):
    outer_count = lax.axis_size("dev")
    pair_count = lax.axis_size("pair")
    core_count = lax.axis_size("sub")
    attended = attend(queries, key_rows, value_rows, states, decay_rates, head_gain)
    partial_value = jnp.dot(
        lax.all_gather(attended, ("dev", "sub"), axis=0, tiled=True),
        out_weight,
        preferred_element_type=jnp.float32,
    )
    local_rows = residual.shape[0]
    columns = partial_value.shape[1]
    blocks = partial_value.reshape(outer_count, pair_count, core_count, local_rows, columns)
    ordered = jnp.transpose(blocks, (1, 0, 2, 3, 4)).reshape(
        pair_count, outer_count * core_count * local_rows, columns
    )
    shared = lax.psum_scatter(ordered, "pair", scatter_dimension=0, tiled=True)
    shared = shared.reshape(outer_count * core_count, local_rows, columns)
    regrouped = lax.all_to_all(shared, ("dev", "sub"), split_axis=0, concat_axis=2, tiled=True)
    own_rows = regrouped[0]
    combined = residual.astype(jnp.float32) + own_rows
    spread = jnp.mean(combined * combined, axis=-1, keepdims=True)
    normed = (combined * lax.rsqrt(spread + EPSILON) * norm_gain).astype(jnp.bfloat16)
    width = normed.shape[1]
    top_count = expert_ids.shape[1]
    expert_count = outer_count // 2
    capacity = max(2, local_rows * top_count // expert_count)
    chosen_ids = expert_ids.reshape(-1)
    choose = (chosen_ids[:, None] == jnp.arange(expert_count, dtype=jnp.int32)[None, :]).astype(
        jnp.int32
    )
    before = jnp.cumsum(choose, axis=0) - choose
    position = jnp.sum(before * choose, axis=1)
    target = chosen_ids * capacity + position
    placing = (
        target[None, :] == jnp.arange(expert_count * capacity, dtype=jnp.int32)[:, None]
    ).astype(jnp.bfloat16)
    repeated = jnp.repeat(normed, top_count, axis=0)
    packed = jnp.dot(placing, repeated, preferred_element_type=jnp.float32).astype(jnp.bfloat16)
    slot_rows = packed.reshape(expert_count, 1, capacity, width)
    outgoing = jnp.broadcast_to(slot_rows, (expert_count, 2, capacity, width)).reshape(
        outer_count, capacity, width
    )
    partials = expert_apply(
        lax.all_gather(
            lax.all_to_all(outgoing, "dev", split_axis=0, concat_axis=0, tiled=True)[None],
            ("pair", "sub"),
            axis=0,
            tiled=True,
        ),
        expert_gate,
        expert_up,
        expert_down,
    )
    summed_terms = lax.psum_scatter(partials, ("pair", "sub"), scatter_dimension=0, tiled=True)
    returned = lax.all_to_all(summed_terms[0], "dev", split_axis=0, concat_axis=0, tiled=True)
    halves = jnp.sum(returned.reshape(expert_count, -1, capacity, width), axis=1).reshape(
        expert_count * capacity, width
    )
    weighting = placing.astype(jnp.float32) * gate_weights.reshape(-1)[None, :]
    per_slot = lax.dot_general(
        weighting,
        halves,
        (((0,), (0,)), ((), ())),
        precision=HIGHEST,
        preferred_element_type=jnp.float32,
    )
    mixture = jnp.sum(per_slot.reshape(local_rows, top_count, width), axis=1)
    return (combined + mixture).astype(jnp.bfloat16)


def solution(mesh):
    return jax.shard_map(
        on_device,
        mesh=mesh,
        in_specs=(
            P(("grp", "dev", "sub"), "pair"),
            P(("grp", "dev", "sub"), "pair"),
            P(("grp", "dev", "sub"), "pair"),
            P(("grp", "dev", "sub"), "pair", None, None),
            P("pair"),
            P("pair"),
            P("pair", ("dev", "sub")),
            P(("grp", "dev", "pair", "sub"), None),
            P(),
            P(("grp", "dev", "pair", "sub"), None),
            P(("grp", "dev", "pair", "sub"), None),
            P(("dev", "pair", "sub"), None),
            P(("dev", "pair", "sub"), None),
            P(("dev", "pair", "sub"), None),
        ),
        out_specs=P(("grp", "dev", "pair", "sub"), None),
        check_vma=False,
    )
```

profile of v0, /device:TPU:0, one launch (start us, length us, event | category | flops | bytes accessed | tf_op | source)
XLA Modules:
  0.0 199.2 jit_solution(17931602684695852897)
XLA Ops:
  6.6 0.8 neg.10
  7.4 1.0 copy.63
  8.3 0.9 copy.64
  9.2 0.9 copy.65
  10.4 4.2 %fusion.2 = f32[4,4,16,128]{3,1,2,0:T(4,128)S(1)} fusion(f32[4,16,128,128]{3,2,1,0:T(8,128)} %param.17, f32[4,16]{0,1:T(8,128)S(1)} %multiply_exponential_fusion, bf16[4,4,16,128]{3,2,1,0:T(8,128)(2,1)S(1)} %bitcast.61), kind=kOutput, calls=%fused_computation.8 | convolution fusion | flops 50364416 | bytes 4391168 | tf_op jit(solution)/shard_map/rphk,rhkv->rphv/dot_general | solution.py:22
  15.1 0.8 multiply_convert_fusion.1
  16.0 16.5 %all_gather.6 = bf16[128,2048]{1,0:T(8,128)(2,1)S(1)} all-gather(bf16[16,2048]{1,0:T(8,128)(2,1)S(1)} %bitcast.63), channel_id=1, replica_groups=mesh['grp'=2,'dev'=8,'pair'=2,'sub'=1] {'dev','sub'}, dimensions={0}, use_global_device_ids=true | all-gather | bytes 589824 | tf_op jit(solution)/shard_map/all_gather | solution.py:74
  33.1 0.8 copy.79
  33.9 0.8 copy.55
  34.7 13.6 %reduce-scatter.3.cloned.1.call-done = f32[1,64,768]{2,1,0:T(8,128)} async-done(((f32[2,64,768]{2,1,0:T(8,128)}), f32[1,64,768]{2,1,0:T(8,128)}) %reduce-scatter.3.cloned.1.call-update) | async-done | bytes 196624 | tf_op jit(solution)/shard_map/reduce_scatter | solution.py:84
  48.3 4.6 %all-to-all-start = ((f32[8,8,768]{2,1,0:T(8,128)}), f32[8,8,768]{2,1,0:T(8,128)S(1)}, u32[]{:S(2)}, u32[]{:S(2)}) async-start(f32[8,8,768]{2,1,0:T(8,128)} %bitcast.65), calls=%async_computation.1 | async-start | bytes 393216 | tf_op jit(solution)/shard_map/all_to_all | solution.py:86
  53.2 8.0 %all-to-all-done = f32[8,8,768]{2,1,0:T(8,128)S(1)} async-done(((f32[8,8,768]{2,1,0:T(8,128)}), f32[8,8,768]{2,1,0:T(8,128)S(1)}, u32[]{:S(2)}, u32[]{:S(2)}) %all-to-all-start) | async-done | bytes 196640 | tf_op jit(solution)/shard_map/all_to_all | solution.py:86
  61.2 1.1 multiply_reduce_fusion
  62.3 1.0 multiply_convert_fusion
  63.3 0.8 broadcast_in_dim.22
  64.1 1.0 reshape.176
  65.1 0.9 convolution_convert_fusion
  65.9 1.0 broadcast_in_dim.23
  67.0 14.9 %all_to_all.25 = bf16[8,4,6144]{2,1,0:T(4,128)(2,1)S(1)} all-to-all(bf16[8,4,6144]{2,1,0:T(4,128)(2,1)S(1)} %bitcast.57), channel_id=1, replica_groups=mesh['grp'=2,'dev'=8,'pair'=2,'sub'=1] {'dev'}, dimensions={0} | all-to-all | bytes 786432 | tf_op jit(solution)/shard_map/all_to_all | solution.py:113
  82.0 11.6 %all-gather = bf16[16,4,6144]{2,1,0:T(4,128)(2,1)} all-gather(bf16[8,4,6144]{2,1,0:T(4,128)(2,1)S(1)} %all_to_all.25), channel_id=2, replica_groups=mesh['grp'=2,'dev'=8,'pair'=2,'sub'=1] {'pair','sub'}, dimensions={0}, use_global_device_ids=true | all-gather | bytes 1179648 | tf_op jit(solution)/shard_map/all_gather | solution.py:112
  93.6 2.3 %reshape.178 = bf16[64,6144]{1,0:T(8,128)(2,1)} reshape(bf16[16,4,6144]{2,1,0:T(4,128)(2,1)} %all-gather) | data formatting | bytes 1572864 | tf_op jit(solution)/shard_map/reshape | solution.py:44
  95.9 10.4 %fusion.27 = f32[64,1152]{1,0:T(8,128)} fusion(bf16[64,6144]{1,0:T(8,128)(2,1)} %reshape.178, bf16[1152,6144]{1,0:T(8,128)(2,1)} %param.25), kind=kOutput, calls=%fused_computation.53 | convolution fusion | flops 905969664 | bytes 15237120 | tf_op jit(solution)/shard_map/dot_general | solution.py:46
  106.3 20.7 %fusion.3 = f32[64,6144]{1,0:T(8,128)} fusion(bf16[1152,6144]{1,0:T(8,128)(2,1)} %param.27, bf16[64,6144]{1,0:T(8,128)(2,1)} %reshape.178, bf16[1152,6144]{1,0:T(8,128)(2,1)} %param.26, f32[64,1152]{1,0:T(8,128)} %fusion.27), kind=kOutput, calls=%fused_computation.10 | convolution fusion | flops 1812381696 | bytes 30965760 | tf_op jit(solution)/shard_map/dot_general | solution.py:49
  127.0 2.8 %reshape.179 = f32[2,8,4,6144]{3,2,1,0:T(4,128)} reshape(f32[64,6144]{1,0:T(8,128)} %fusion.3) | data formatting | bytes 3145728 | tf_op jit(solution)/shard_map/reshape | solution.py:50
  129.7 3.5 %copy.58 = f32[2,8,4,6144]{3,1,2,0:T(8,128)} copy(f32[2,8,4,6144]{3,2,1,0:T(4,128)} %reshape.179) | data formatting | bytes 3145728 | tf_op jit(solution)/shard_map/reshape | solution.py:50
  133.2 24.6 %reduce-scatter.5.cloned.1.call-done = f32[1,8,4,6144]{3,1,2,0:T(8,128)} async-done(((f32[2,8,4,6144]{3,1,2,0:T(8,128)}), f32[1,8,4,6144]{3,1,2,0:T(8,128)}) %reduce-scatter.5.cloned.1.call-update) | async-done | bytes 786448 | tf_op jit(solution)/shard_map/reduce_scatter | solution.py:122
  157.9 2.5 %copy.59 = f32[8,4,6144]{2,1,0:T(4,128)} copy(f32[8,4,6144]{2,0,1:T(8,128)} %bitcast.59) | data formatting | bytes 1572864 | tf_op jit(solution)/shard_map/squeeze | solution.py:123
  160.4 4.6 %all-to-all-start.2 = ((f32[8,4,6144]{2,1,0:T(4,128)}), f32[8,4,6144]{2,1,0:T(4,128)}, u32[]{:S(2)}, u32[]{:S(2)}) async-start(f32[8,4,6144]{2,1,0:T(4,128)} %copy.59), calls=%async_computation.4 | async-start | bytes 1572864 | tf_op jit(solution)/shard_map/all_to_all | solution.py:123
  165.2 20.9 %all-to-all-done.2 = f32[8,4,6144]{2,1,0:T(4,128)} async-done(((f32[8,4,6144]{2,1,0:T(4,128)}), f32[8,4,6144]{2,1,0:T(4,128)}, u32[]{:S(2)}, u32[]{:S(2)}) %all-to-all-start.2) | async-done | bytes 786464 | tf_op jit(solution)/shard_map/all_to_all | solution.py:123
  186.1 2.1 %bitcast_reduce_fusion = f32[4,4,6144]{2,1,0:T(4,128)} fusion(f32[8,4,6144]{2,1,0:T(4,128)} %all-to-all-done.2), kind=kLoop, calls=%fused_computation.9 | loop fusion | flops 98304 | bytes 1179648 | tf_op jit(solution)/shard_map/reduce_sum | solution.py:124
  188.2 1.9 reshape.184
  190.1 1.6 convolution_reduce_fusion
  (32 shorter events, 2.9 us)
Async XLA Ops:
  6.5 26.0 %copy-start = (bf16[2048,768]{1,0:T(8,128)(2,1)S(1)}, bf16[2048,768]{1,0:T(8,128)(2,1)}, u32[]{:S(2)}) copy-start(bf16[2048,768]{1,0:T(8,128)(2,1)} %param.20) | copy-start | bytes 9437188
  6.5 41.7 %reduce-scatter.3.cloned.1.call-start = ((), (), s32[]{:S(2)}) async-start(), calls=%async_computation.5 | async-start | bytes 589824 | tf_op jit(solution)/shard_map/reduce_scatter | solution.py:84
  48.3 12.9 %all-to-all-start = ((f32[8,8,768]{2,1,0:T(8,128)}), f32[8,8,768]{2,1,0:T(8,128)S(1)}, u32[]{:S(2)}, u32[]{:S(2)}) async-start(f32[8,8,768]{2,1,0:T(8,128)} %bitcast.65), calls=%async_computation.1 | async-start | bytes 393216 | tf_op jit(solution)/shard_map/all_to_all | solution.py:86
  52.9 105.0 %reduce-scatter.5.cloned.1.call-start = ((), (), s32[]{:S(2)}) async-start(), calls=%async_computation.6 | async-start | bytes 2359296 | tf_op jit(solution)/shard_map/reduce_scatter | solution.py:122
  106.3 83.8 %copy-start.2 = (f32[8,2]{0,1:T(2,128)S(1)}, f32[8,2]{0,1:T(2,128)}, u32[]{:S(2)}) copy-start(f32[8,2]{0,1:T(2,128)} %param.24) | copy-start | bytes 196
  106.3 85.4 %copy-start.1 = (bf16[8,6144]{1,0:T(8,128)(2,1)S(1)}, bf16[8,6144]{1,0:T(8,128)(2,1)}, u32[]{:S(2)}) copy-start(bf16[8,6144]{1,0:T(8,128)(2,1)} %param.21) | copy-start | bytes 294916
  160.4 25.7 %all-to-all-start.2 = ((f32[8,4,6144]{2,1,0:T(4,128)}), f32[8,4,6144]{2,1,0:T(4,128)}, u32[]{:S(2)}, u32[]{:S(2)}) async-start(f32[8,4,6144]{2,1,0:T(4,128)} %copy.59), calls=%async_computation.4 | async-start | bytes 1572864 | tf_op jit(solution)/shard_map/all_to_all | solution.py:123
Sparse Core Ops, SparseCore 0:
  34.0 14.2 reduce-scatter.2
  133.4 24.4 reduce-scatter.4
where the time goes:
time: 200 us; the launch traced here: 199 us
  waiting for transfers between devices  67.1 us (34%)
  blocking collectives  43 us (22%)
  matrix products  38.9 us (19%)
  local copies, waits for them, and re-layouts  20.3 us (10%)
  between operations  13.5 us (7%)
  starting transfers between devices  9.27 us (5%)
  other arithmetic  7.04 us (4%)
    reduce_scatter x1, waiting for transfers between devices, on_device(): lax.psum_scatter(partials, ('pair', 'sub'), scatter_dimension=0, tiled=True)  24.6 us
    all_to_all x1, waiting for transfers between devices, on_device(): lax.all_to_all(summed_terms[0], 'dev', split_axis=0, concat_axis=0, tiled...  20.9 us
    dot_general x1, matrix products, expert_apply(): output = jnp.dot(hidden, down_part, preferred_element_type=jnp.float32)  20.7 us
    all_gather x1, blocking collectives, on_device(): lax.all_gather(attended, ('dev', 'sub'), axis=0, tiled=True)  16.5 us
    all_to_all x1, blocking collectives, on_device(): lax.all_to_all(outgoing, 'dev', split_axis=0, concat_axis=0, tiled=True)  14.9 us
    reduce_scatter x1, waiting for transfers between devices, on_device(): shared = lax.psum_scatter(ordered, 'pair', scatter_dimension=0, tiled=True)  13.6 us
    all_gather x1, blocking collectives, on_device(): lax.all_gather(lax.all_to_all(outgoing, 'dev', split_axis=0, concat_axis=...  11.6 us
    dot_general x1, matrix products, expert_apply(): lax.dot_general(flattened, gate_part, contract, preferred_element_type=jn...  10.4 us
  transfers between devices with their start and end apart: 4, of which 4 were waited for; matrix products, arithmetic and copies ran while one was open for 1% of the time, Pallas kernels for 0%

commit v1 on v0

--- a/solution.py
+++ b/solution.py
@@ -1,6 +1,10 @@
+import functools
+
 import jax
 import jax.numpy as jnp
 from jax import lax
+from jax.experimental import pallas as pl
+from jax.experimental.pallas import tpu as pltpu
 from jax.sharding import PartitionSpec as P
 
 EPSILON = 1e-06
@@ -135,10 +139,553 @@
     mixture = jnp.sum(per_slot.reshape(local_rows, top_count, width), axis=1)
     return (combined + mixture).astype(jnp.bfloat16)
 
+MESH = pl.DeviceIdType.MESH
+VMEM_BYTES = 67043328
+TRANSPOSED = (((1,), (1,)), ((), ()))
+LEADING = (((0,), (0,)), ((), ()))
+
+
+def plan_fits(mesh):
+    sizes = mesh.shape
+    return sizes["sub"] == 1 and sizes["pair"] == 2 and sizes["dev"] % 2 == 0 and sizes["dev"] > 2
+
+
+def layer_kernel(
+    outer_count,
+    queries_hbm,
+    keys_hbm,
+    values_hbm,
+    states_hbm,
+    decay_ref,
+    head_gain_hbm,
+    out_weight_hbm,
+    residual_hbm,
+    norm_gain_hbm,
+    ids_hbm,
+    gates_hbm,
+    gate_hbm,
+    up_hbm,
+    down_hbm,
+    out_ref,
+    queries,
+    keys,
+    values,
+    states,
+    head_gain,
+    out_weight,
+    residual,
+    norm_gain,
+    ids,
+    gates,
+    gate,
+    up,
+    down,
+    gathered,
+    terms,
+    terms_in,
+    combined,
+    packed,
+    routed,
+    gate_sum,
+    up_sum,
+    hidden,
+    partial,
+    core_out,
+    core_in,
+    pair_out,
+    pair_in,
+    owner_out,
+    owner_in,
+    local_sem,
+    gather_send,
+    gather_recv,
+    terms_send,
+    terms_recv,
+    route_send,
+    route_recv,
+    core_send,
+    core_recv,
+    pair_send,
+    pair_recv,
+    owner_send,
+    owner_recv,
+):
+    dev = lax.axis_index("dev")
+    pair = lax.axis_index("pair")
+    plane = dev // 2
+    core = dev % 2
+    planes = outer_count // 2
+    total = outer_count * 2
+    me = dev * 2 + pair
+    other_core = {"dev": plane * 2 + 1 - core, "pair": pair}
+    other_pair = {"dev": dev, "pair": 1 - pair}
+    started = []
+
+    def send(source, target, send_sem, recv_sem, where):
+        copy = pltpu.make_async_remote_copy(
+            src_ref=source,
+            dst_ref=target,
+            send_sem=send_sem,
+            recv_sem=recv_sem,
+            device_id=where,
+            device_id_type=MESH,
+        )
+        copy.start()
+        started.append(copy)
+
+    def arrived(target, send_sem, recv_sem):
+        pltpu.make_async_remote_copy(
+            src_ref=target,
+            dst_ref=target,
+            send_sem=send_sem,
+            recv_sem=recv_sem,
+            device_id=other_core,
+            device_id_type=MESH,
+        ).wait_recv()
+
+    loads = [
+        pltpu.make_async_copy(source, target, local_sem.at[number])
+        for number, (source, target) in enumerate(
+            [
+                (queries_hbm, queries),
+                (keys_hbm, keys),
+                (values_hbm, values),
+                (states_hbm, states),
+                (head_gain_hbm, head_gain),
+                (ids_hbm, ids),
+                (gates_hbm, gates),
+                (residual_hbm, residual),
+                (norm_gain_hbm, norm_gain),
+                (out_weight_hbm, out_weight),
+                (gate_hbm, gate),
+                (up_hbm, up),
+                (down_hbm, down),
+            ]
+        )
+    ]
+    for load in loads:
+        load.start()
+    barrier = pltpu.get_barrier_semaphore()
+    for offset in range(1, total):
+        peer = lax.rem(me + offset, total)
+        pl.semaphore_signal(
+            barrier, inc=1, device_id={"dev": peer // 2, "pair": peer % 2}, device_id_type=MESH
+        )
+    for load in loads[:5]:
+        load.wait()
+
+    requests, heads, size, _ = states.shape
+    rows = queries.shape[0]
+    positions = rows // requests
+    groups = gathered.shape[0]
+    group_heads = heads // groups
+    row_at = lax.broadcasted_iota(jnp.int32, (rows, rows), 0)
+    column_at = lax.broadcasted_iota(jnp.int32, (rows, rows), 1)
+    seen = (row_at // positions == column_at // positions) & (column_at <= row_at)
+    distance = jnp.maximum(row_at - column_at, 0).astype(jnp.float32)
+    wide_row = lax.broadcasted_iota(jnp.int32, (rows, size), 0)
+    steps = (wide_row % positions + 1).astype(jnp.float32)
+
+    def one_head(head):
+        columns = pl.ds(head * size, size)
+        query = queries[:, columns]
+        value = values[:, columns]
+        rate = decay_ref[head]
+        scores = lax.dot_general(
+            query, keys[:, columns], TRANSPOSED, preferred_element_type=jnp.float32
+        )
+        scores = jnp.where(seen, scores * jnp.exp(-rate * distance), 0.0)
+        mixed = jnp.zeros((rows, size), jnp.float32)
+        query_float = query.astype(jnp.float32)
+        for request in range(requests):
+            own = jnp.where(wide_row // positions == request, query_float, 0.0)
+            mixed = mixed + jnp.dot(
+                own.astype(jnp.bfloat16),
+                states[request, head].astype(jnp.bfloat16),
+                preferred_element_type=jnp.float32,
+            )
+        mixed = mixed * jnp.exp(-rate * steps) + jnp.dot(
+            scores.astype(jnp.bfloat16), value, preferred_element_type=jnp.float32
+        )
+        spread = jnp.mean(mixed * mixed, axis=1, keepdims=True)
+        return (mixed * lax.rsqrt(spread + EPSILON) * head_gain[:, columns]).astype(jnp.bfloat16)
+
+    for group in range(groups):
+        for inner in range(group_heads):
+            gathered[group, dev, :, inner * size : (inner + 1) * size] = one_head(
+                group * group_heads + inner
+            )
+        if group == 0:
+            pl.semaphore_wait(barrier, total - 1)
+        mine = gathered.at[group, dev]
+        for offset in range(1, planes):
+            where = {"dev": lax.rem(plane + offset, planes) * 2 + core, "pair": pair}
+            send(mine, mine, gather_send.at[group, offset], gather_recv.at[group, dev], where)
+        send(mine, mine, gather_send.at[group, 0], gather_recv.at[group, dev], other_core)
+
+    loads[9].wait()
+    width = gathered.shape[3]
+    projected = None
+    for group in range(groups):
+        for offset in range(1, planes):
+            source = lax.rem(plane + planes - offset, planes) * 2 + core
+            block = gathered.at[group, source]
+            arrived(block, gather_send.at[group, 0], gather_recv.at[group, source])
+            send(
+                block,
+                block,
+                gather_send.at[group, planes + offset],
+                gather_recv.at[group, source],
+                other_core,
+            )
+    for group in range(groups):
+        for offset in range(planes):
+            source = lax.rem(plane + planes - offset, planes) * 2 + 1 - core
+            arrived(
+                gathered.at[group, source],
+                gather_send.at[group, 0],
+                gather_recv.at[group, source],
+            )
+        product = jnp.dot(
+            gathered[group].reshape(outer_count * rows, width),
+            out_weight[group * width : (group + 1) * width, :],
+            preferred_element_type=jnp.float32,
+        )
+        projected = product if projected is None else projected + product
+    local_rows = residual.shape[0]
+    columns = out_weight.shape[1]
+    terms[...] = projected.reshape(total, local_rows, columns).astype(jnp.bfloat16)
+    for offset in range(1, total):
+        owner = lax.rem(me + offset, total)
+        send(
+            terms.at[owner],
+            terms_in.at[me],
+            terms_send.at[offset],
+            terms_recv.at[me],
+            {"dev": owner // 2, "pair": owner % 2},
+        )
+    terms_in[me] = terms[me]
+
+    for load in loads[5:9]:
+        load.wait()
+    top_count = ids.shape[1]
+    capacity = packed.shape[2]
+    slots = planes * capacity
+    slot_at = lax.broadcasted_iota(jnp.int32, (local_rows, slots), 1)
+    chosen = jnp.zeros((local_rows, slots), jnp.float32)
+    weights = jnp.zeros((local_rows, slots), jnp.float32)
+    for top in range(top_count):
+        named = ids[:, top : top + 1] == slot_at // capacity
+        chosen = chosen + jnp.where(named, 1.0, 0.0)
+        weights = weights + jnp.where(named, gates[:, top : top + 1], 0.0)
+    earlier = jnp.where(
+        lax.broadcasted_iota(jnp.int32, (local_rows, local_rows), 1)
+        < lax.broadcasted_iota(jnp.int32, (local_rows, local_rows), 0),
+        1.0,
+        0.0,
+    )
+    rank = jnp.dot(
+        earlier.astype(jnp.bfloat16),
+        chosen.astype(jnp.bfloat16),
+        preferred_element_type=jnp.float32,
+    )
+    placed = jnp.abs(rank - (slot_at % capacity).astype(jnp.float32)) < 0.5
+    placing = jnp.where(placed, chosen, 0.0)
+    weights = jnp.where(placed, weights, 0.0)
+    weights_high = weights.astype(jnp.bfloat16)
+    weights_low = (weights - weights_high.astype(jnp.float32)).astype(jnp.bfloat16)
+
+    for offset in range(1, total):
+        source = lax.rem(me + total - offset, total)
+        arrived(terms_in.at[source], terms_send.at[1], terms_recv.at[source])
+    squares = jnp.zeros((local_rows, 1), jnp.float32)
+    for part in range(outer_count):
+        span = slice(part * columns, (part + 1) * columns)
+        value = (
+            residual[:, span].astype(jnp.float32)
+            + terms_in[part * 2].astype(jnp.float32)
+            + terms_in[part * 2 + 1].astype(jnp.float32)
+        )
+        combined[:, span] = value
+        squares = squares + jnp.sum(value * value, axis=1, keepdims=True)
+    features = combined.shape[1]
+    scale = lax.rsqrt(squares / features + EPSILON)
+
+    pieces = packed.shape[0]
+    piece = features // pieces
+    placing = placing.astype(jnp.bfloat16)
+
+    def slot_of(from_core, from_pair, from_plane):
+        return (from_core * 2 + from_pair) * planes + from_plane
+
+    my_slot = slot_of(core, pair, plane)
+    for number in range(pieces):
+        span = slice(number * piece, (number + 1) * piece)
+        normed = (combined[:, span] * scale * norm_gain[:, span]).astype(jnp.bfloat16)
+        rows_of = lax.dot_general(placing, normed, LEADING, preferred_element_type=jnp.float32)
+        packed[number] = rows_of.reshape(planes, capacity, piece).astype(jnp.bfloat16)
+        routed[number, my_slot] = packed[number, plane]
+        for offset in range(1, planes):
+            expert = lax.rem(plane + offset, planes)
+            send(
+                packed.at[number, expert],
+                routed.at[number, my_slot],
+                route_send.at[number, offset],
+                route_recv.at[number, my_slot],
+                {"dev": expert * 2 + core, "pair": pair},
+            )
+
+    def relay_first(number):
+        for offset in range(planes):
+            slot = slot_of(core, pair, lax.rem(plane + planes - offset, planes))
+            block = routed.at[number, slot]
+            came = route_recv.at[number, slot]
+            if offset:
+                arrived(block, route_send.at[number, 0], came)
+            send(block, block, route_send.at[number, planes + offset], came, other_pair)
+            send(block, block, route_send.at[number, 2 * planes + offset], came, other_core)
+
+    def relay_second(number):
+        for offset in range(planes):
+            slot = slot_of(core, 1 - pair, lax.rem(plane + planes - offset, planes))
+            block = routed.at[number, slot]
+            came = route_recv.at[number, slot]
+            arrived(block, route_send.at[number, 0], came)
+            send(block, block, route_send.at[number, 3 * planes + offset], came, other_core)
+        for offset in range(2 * planes):
+            slot = slot_of(
+                1 - core, offset // planes, lax.rem(plane + planes - offset % planes, planes)
+            )
+            arrived(routed.at[number, slot], route_send.at[number, 0], route_recv.at[number, slot])
+
+    units = gate.shape[0]
+    tile = 128
+    slot_rows = total * capacity
+
+    def lift(number):
+        span = slice(number * piece, (number + 1) * piece)
+        picked = routed[number].reshape(slot_rows, piece)
+
+        def body(step, carry):
+            part = pl.ds(pl.multiple_of(step * tile, tile), tile)
+            first = lax.dot_general(
+                gate[part, span], picked, TRANSPOSED, preferred_element_type=jnp.float32
+            )
+            second = lax.dot_general(
+                up[part, span], picked, TRANSPOSED, preferred_element_type=jnp.float32
+            )
+            if number:
+                first = first + gate_sum[part, :]
+                second = second + up_sum[part, :]
+            if number < pieces - 1:
+                gate_sum[part, :] = first
+                up_sum[part, :] = second
+            else:
+                hidden[part, :] = (first / (1.0 + jnp.exp(-first)) * second).astype(jnp.bfloat16)
+            return carry
+
+        lax.fori_loop(0, units // tile, body, 0)
+
+    relay_first(0)
+    relay_second(0)
+    for number in range(pieces):
+        if number + 1 < pieces:
+            relay_first(number + 1)
+        if number == 0:
+            loads[10].wait()
+            loads[11].wait()
+        lift(number)
+        if number + 1 < pieces:
+            relay_second(number + 1)
+    loads[12].wait()
+
+    chunks = core_out.shape[0]
+    chunk = features // chunks
+    half = slot_rows // 2
+    quarter = half // 2
+    kept = core * half
+    narrow = chunk // 3 if chunk % 384 == 0 else chunk
+
+    def stage_down(number):
+        def body(step, carry):
+            part = pl.ds(pl.multiple_of(number * chunk + step * narrow, 128), narrow)
+            partial[:, part] = lax.dot_general(
+                hidden[...], down[:, part], LEADING, preferred_element_type=jnp.float32
+            )
+            return carry
+
+        lax.fori_loop(0, chunk // narrow, body, 0)
+        span = slice(number * chunk, (number + 1) * chunk)
+        core_out[number] = partial[pl.ds(half - kept, half), span].astype(jnp.bfloat16)
+        send(
+            core_out.at[number],
+            core_in.at[number],
+            core_send.at[number],
+            core_recv.at[number],
+            other_core,
+        )
+
+    def chip_sum(number, which):
+        span = slice(number * chunk, (number + 1) * chunk)
+        return partial[pl.ds(kept + which * quarter, quarter), span] + core_in[
+            number, pl.ds(which * quarter, quarter), :
+        ].astype(jnp.float32)
+
+    def stage_core(number):
+        arrived(core_in.at[number], core_send.at[number], core_recv.at[number])
+        pair_out[number] = chip_sum(number, 1 - pair).astype(jnp.bfloat16)
+        send(
+            pair_out.at[number],
+            pair_in.at[number],
+            pair_send.at[number],
+            pair_recv.at[number],
+            other_pair,
+        )
+
+    def stage_pair(number):
+        arrived(pair_in.at[number], pair_send.at[number], pair_recv.at[number])
+        value = chip_sum(number, pair) + pair_in[number].astype(jnp.float32)
+        owner_out[number] = value.reshape(planes, capacity, chunk).astype(jnp.bfloat16)
+        owner_in[number, plane] = owner_out[number, plane]
+        for offset in range(1, planes):
+            owner = lax.rem(plane + offset, planes)
+            send(
+                owner_out.at[number, owner],
+                owner_in.at[number, plane],
+                owner_send.at[number, offset],
+                owner_recv.at[number, plane],
+                {"dev": owner * 2 + core, "pair": pair},
+            )
+
+    def stage_owner(number):
+        for offset in range(1, planes):
+            expert = lax.rem(plane + planes - offset, planes)
+            arrived(
+                owner_in.at[number, expert],
+                owner_send.at[number, offset],
+                owner_recv.at[number, expert],
+            )
+        span = slice(number * chunk, (number + 1) * chunk)
+        result = owner_in[number].reshape(slots, chunk)
+        mixture = jnp.dot(weights_high, result, preferred_element_type=jnp.float32) + jnp.dot(
+            weights_low, result, preferred_element_type=jnp.float32
+        )
+        out_ref[:, span] = (combined[:, span] + mixture).astype(jnp.bfloat16)
+
+    for step in range(chunks + 3):
+        if step < chunks:
+            stage_down(step)
+        if 0 <= step - 1 < chunks:
+            stage_core(step - 1)
+        if 0 <= step - 2 < chunks:
+            stage_pair(step - 2)
+        if 0 <= step - 3 < chunks:
+            stage_owner(step - 3)
+    for copy in started:
+        copy.wait_send()
+
+
+def fused_on_device(
+    queries,
+    key_rows,
+    value_rows,
+    states,
+    decay_rates,
+    head_gain,
+    out_weight,
+    residual,
+    norm_gain,
+    expert_ids,
+    gate_weights,
+    expert_gate,
+    expert_up,
+    expert_down,
+):
+    outer_count = lax.axis_size("dev")
+    planes = outer_count // 2
+    total = outer_count * 2
+    rows, head_width = queries.shape
+    requests, heads, size, _ = states.shape
+    local_rows, features = residual.shape
+    columns = out_weight.shape[1]
+    units = expert_gate.shape[0]
+    capacity = max(2, local_rows * expert_ids.shape[1] // planes)
+    slot_rows = total * capacity
+    groups = 4
+    pieces = 2
+    chunks = 4
+    width = head_width // groups
+    piece = features // pieces
+    chunk = features // chunks
+    half = slot_rows // 2
+    low = jnp.bfloat16
+    operands = [
+        queries,
+        key_rows,
+        value_rows,
+        states,
+        decay_rates,
+        head_gain.reshape(1, head_width),
+        out_weight,
+        residual,
+        norm_gain.reshape(1, features),
+        expert_ids,
+        gate_weights,
+        expert_gate,
+        expert_up,
+        expert_down,
+    ]
+    anywhere = pl.BlockSpec(memory_space=pl.ANY)
+    in_specs = [anywhere] * len(operands)
+    in_specs[4] = pl.BlockSpec(memory_space=pltpu.SMEM)
+    staged = [pltpu.VMEM(x.shape, x.dtype) for i, x in enumerate(operands) if i != 4]
+    dma = pltpu.SemaphoreType.DMA
+    return pl.pallas_call(
+        functools.partial(layer_kernel, outer_count),
+        out_shape=jax.ShapeDtypeStruct((local_rows, features), low),
+        in_specs=in_specs,
+        out_specs=pl.BlockSpec(memory_space=pltpu.VMEM),
+        scratch_shapes=staged
+        + [
+            pltpu.VMEM((groups, outer_count, rows, width), low),
+            pltpu.VMEM((total, local_rows, columns), low),
+            pltpu.VMEM((total, local_rows, columns), low),
+            pltpu.VMEM((local_rows, features), jnp.float32),
+            pltpu.VMEM((pieces, planes, capacity, piece), low),
+            pltpu.VMEM((pieces, total, capacity, piece), low),
+            pltpu.VMEM((units, slot_rows), jnp.float32),
+            pltpu.VMEM((units, slot_rows), jnp.float32),
+            pltpu.VMEM((units, slot_rows), low),
+            pltpu.VMEM((slot_rows, features), jnp.float32),
+            pltpu.VMEM((chunks, half, chunk), low),
+            pltpu.VMEM((chunks, half, chunk), low),
+            pltpu.VMEM((chunks, half // 2, chunk), low),
+            pltpu.VMEM((chunks, half // 2, chunk), low),
+            pltpu.VMEM((chunks, planes, capacity, chunk), low),
+            pltpu.VMEM((chunks, planes, capacity, chunk), low),
+            dma((len(operands) - 1,)),
+            dma((groups, 2 * planes)),
+            dma((groups, outer_count)),
+            dma((total,)),
+            dma((total,)),
+            dma((pieces, 4 * planes)),
+            dma((pieces, total)),
+            dma((chunks,)),
+            dma((chunks,)),
+            dma((chunks,)),
+            dma((chunks,)),
+            dma((chunks, planes)),
+            dma((chunks, planes)),
+        ],
+        compiler_params=pltpu.CompilerParams(
+            collective_id=0, has_side_effects=True, vmem_limit_bytes=VMEM_BYTES
+        ),
+    )(*operands)
+
 
 def solution(mesh):
     return jax.shard_map(
-        on_device,
+        fused_on_device if plan_fits(mesh) else on_device,
         mesh=mesh,
         in_specs=(
             P(("grp", "dev", "sub"), "pair"),

time: 200 us -> 65.5 us (0.33)
  waiting for transfers between devices: 67.1 us -> 0 us
  Pallas kernels: 0 us -> 61 us
  blocking collectives: 43 us -> 0 us
  matrix products: 38.9 us -> 0 us
  local copies, waits for them, and re-layouts: 20.3 us -> 4.23 us
  between operations: 13.5 us -> 0.01 us
  starting transfers between devices: 9.27 us -> 0 us
  other arithmetic: 7.04 us -> 0 us
    pallas_call x0 -> x1, Pallas kernels: none -> 61 us  [fused_on_device(): pl.pallas_call(functools.partial(layer_kernel, outer_count), out_shape=ja...]
    dot_general x8 -> x0, matrix products: 38.9 us -> none  [the longest x1 20.7 us: expert_apply(): output = jnp.dot(hidden, down_part, preferred_element_type=jnp.float32)]
    reduce_scatter x2 -> x0, waiting for transfers between devices: 38.2 us -> none  [the longest x1 24.6 us: on_device(): lax.psum_scatter(partials, ('pair', 'sub'), scatter_dimension=0, tiled=True)]
    all_to_all x2 -> x0, waiting for transfers between devices: 28.8 us -> none  [the longest x1 20.9 us: on_device(): lax.all_to_all(summed_terms[0], 'dev', split_axis=0, concat_axis=0, tiled...]
    all_gather x2 -> x0, blocking collectives: 28.1 us -> none  [the longest x1 16.5 us: on_device(): lax.all_gather(attended, ('dev', 'sub'), axis=0, tiled=True)]
    all_to_all x1 -> x0, blocking collectives: 14.9 us -> none  [on_device(): lax.all_to_all(outgoing, 'dev', split_axis=0, concat_axis=0, tiled=True)]
    reshape x7 -> x0, local copies, waits for them, and re-layouts: 12.3 us -> none  [the longest x2 6.26 us: expert_apply(): return output.reshape(leading)]
    all_to_all x2 -> x0, starting transfers between devices: 9.23 us -> none  [the longest x1 4.63 us: on_device(): lax.all_to_all(shared, ('dev', 'sub'), split_axis=0, concat_axis=2, tiled...]
  transfers between devices with their start and end apart: 4 -> 0, of which waited for: 4 -> 0; matrix products, arithmetic and copies ran while one was open for 1% -> 0% of each run, Pallas kernels for 0% -> 0%
where the time goes in v1:
time: 65.5 us; the launch traced here: 65.3 us
  Pallas kernels  61 us (93%)
  local copies, waits for them, and re-layouts  4.23 us (6%)
    pallas_call x1, Pallas kernels, fused_on_device(): pl.pallas_call(functools.partial(layer_kernel, outer_count), out_shape=ja...  61 us
    unnamed x3, local copies, waits for them, and re-layouts  4.23 us

profile of v1, /device:TPU:0, one launch (start us, length us, event | category | flops | bytes accessed | tf_op | source)
XLA Modules:
  0.0 65.3 jit_solution(1048527007812683253)
XLA Ops:
  0.0 1.3 %copy.15.ids_hbm = s32[8,2]{1,0:T(8,128)} copy(s32[8,2]{0,1:T(2,128)} %param.23) | data formatting | bytes 128 | tf_op args[9]
  1.3 1.3 %copy.16.gates_hbm = f32[8,2]{1,0:T(8,128)} copy(f32[8,2]{0,1:T(2,128)} %param.24) | data formatting | bytes 128 | tf_op args[10]
  2.7 61.0 %shard_map.136 = bf16[8,6144]{1,0:T(8,128)(2,1)} custom-call(bf16[16,2048]{1,0:T(8,128)(2,1)} %queries_hbm.1, bf16[16,2048]{1,0:T(8,128)(2,1)} %keys_hbm.1, bf16[16,2048]{1,0:T(8,128)(2,1)} %values_hbm.1, f32[4,16,128,128]{3,2,1,0:T(8,128)} %states_hbm.1, f32[16]{0:T(128)} %decay_ref.1, f32[1,2048]{1,0:T(1,128)} %bitcast.3, ...), custom_call_target="tpu_custom_call" | custom-call | tf_op jit(solution)/shard_map/pallas_call | solution.py:643
  63.7 1.5 %copy.18 = bf16[8,6144]{1,0:T(8,128)(2,1)} copy(bf16[8,6144]{1,0:T(8,128)(2,1)} %shard_map.136) | data formatting | bytes 196608
